TPU v7x, 512 devices: a whole 4x8x8 slice. The times are simulated.
512 devices in a mesh: dom: 128 (over z, y, core), rep: 4 (over x).
Axes of the slice: x: 4, y: 8, z: 8, core: 2. Of those that a mesh axis runs over, the one named last changes fastest.
Arguments:
- embedding: bfloat16 [131072, 128], P('dom'), may hold values from -6 to 6
- cotangent: bfloat16 [131072, 128], P('dom'), may hold values from -6 to 6
- degrees: int32 [131072], P('dom'), may hold values from 2 to 64
- tile_values: bfloat16 [128, 4, 32, 128, 128], P('dom', 'rep'), may hold values from 0 to 2, as said below
- tile_target: int32 [128, 4, 32], P('dom', 'rep'), may hold values from 0 to 7
- tile_source: int32 [128, 4, 32], P('dom', 'rep'), may hold values from 0 to 27
- live_tile_count: int32 [128, 4], P('dom', 'rep'), may hold values from 4 to 32, as said below
- send_rows: int32 [128, 128, 16], P('dom'), may hold values from 0 to 1023
- hub_rows: int32 [128, 4], P('dom'), may hold values from 0 to 1023
Outputs:
- layer_output: bfloat16 [131072, 128], P(('dom', 'rep'))
- embedding_gradient: bfloat16 [131072, 128], P(('dom', 'rep'))
Inputs may be any that keep to these rules, and one draw needn't show every extreme that they name: `tile_values`: each entry is an edge weight, zero where the two nodes share no edge. `live_tile_count`: slots at or past a device's count are not live; in every draw some device has all 32 slots live.
All inputs are finite; a program needn't handle non-finite values.
Results may differ from a plain program's by a relative error of at most 0.0048.
Values may be sent and summed in bfloat16 or wider, within the bound.
No kernel may reach another device: no remote copies, remote signals or barrier semaphores. Data moves between devices by JAX's collectives and lax.ppermute only.
A program may use at most 64 MiB of HBM per device.

v0:
```python
import jax
import jax.numpy as jnp
from jax import lax
from jax.sharding import PartitionSpec as P


def body(
    embedding,
    cotangent,
    degrees,
    tile_values,
    tile_target,
    tile_source,
    live_tile_count,
    send_rows,
    hub_rows,
):
    own_rows, feature_width = embedding.shape
    tile_size = tile_values.shape[-1]
    slot_grand_total = tile_values.shape[2]
    partitions = send_rows.shape[1]
    pair_rows = send_rows.shape[2]
    replicas = lax.axis_size("rep")
    replica_index = lax.axis_index("rep")
    root_inverse = lax.rsqrt(degrees.astype(jnp.float32))
    scaled = (root_inverse[:, None] * embedding.astype(jnp.float32)).astype(jnp.bfloat16)
    weighted = (root_inverse[:, None] * cotangent.astype(jnp.float32)).astype(jnp.bfloat16)
    arrived = lax.all_to_all(scaled[send_rows[0]], "dom", split_axis=0, concat_axis=0, tiled=True)
    hub_block = lax.all_gather(scaled[hub_rows[0]], "dom", axis=0, tiled=True)
    source = jnp.concatenate([scaled, arrived.reshape(-1, feature_width), hub_block], 0)
    source_blocks = source.shape[0] // tile_size
    source = source.reshape(source_blocks, tile_size, feature_width)
    target_blocks = own_rows // tile_size
    tile_matrix_block = tile_values[0, 0]
    targets = tile_target[0, 0]
    sources = tile_source[0, 0]
    tile_alive_mask = (
        jnp.arange(slot_grand_total, dtype=jnp.int32) < live_tile_count[0, 0]
    ).astype(jnp.float32)
    message_product = jnp.einsum(
        "ack,aky->acy", tile_matrix_block, source[sources], preferred_element_type=jnp.float32
    )
    target_onehot = (
        targets[None, :] == jnp.arange(target_blocks, dtype=jnp.int32)[:, None]
    ).astype(jnp.float32) * tile_alive_mask[None, :]
    forward = jnp.dot(
        target_onehot,
        message_product.reshape(slot_grand_total, -1),
        precision=lax.Precision.HIGHEST,
    )
    forward = forward.reshape(own_rows, feature_width)
    weighted_blocks = weighted.reshape(target_blocks, tile_size, feature_width)
    gathered_portion = jnp.einsum(
        "vzr,vzu->vru",
        tile_matrix_block,
        weighted_blocks[targets],
        preferred_element_type=jnp.float32,
    )
    source_onehot = (
        sources[None, :] == jnp.arange(source_blocks, dtype=jnp.int32)[:, None]
    ).astype(jnp.float32) * tile_alive_mask[None, :]
    slot_sums = jnp.dot(
        source_onehot,
        gathered_portion.reshape(slot_grand_total, -1),
        precision=lax.Precision.HIGHEST,
    )
    slot_sums = slot_sums.reshape(-1, feature_width)
    boundary_end = own_rows + partitions * pair_rows
    local_part = slot_sums[:own_rows]
    boundary_part = slot_sums[own_rows:boundary_end].reshape(partitions, pair_rows, feature_width)
    hub_part = slot_sums[boundary_end:]
    returned = lax.all_to_all(boundary_part, "dom", split_axis=0, concat_axis=0, tiled=True)
    gradient_part = local_part.at[send_rows[0]].add(returned)
    hub_total = lax.psum_scatter(hub_part, "dom", scatter_dimension=0, tiled=True)
    gradient_part = gradient_part.at[hub_rows[0]].add(hub_total)
    forward_sum, gradient_sum = (
        lax.psum_scatter(forward, "rep", scatter_dimension=0, tiled=True),
        lax.psum_scatter(gradient_part, "rep", scatter_dimension=0, tiled=True),
    )
    out_rows = own_rows // replicas
    my_root = lax.dynamic_slice_in_dim(root_inverse, replica_index * out_rows, out_rows, 0)
    layer_output = (my_root[:, None] * forward_sum).astype(jnp.bfloat16)
    embedding_gradient = (my_root[:, None] * gradient_sum).astype(jnp.bfloat16)
    return (layer_output, embedding_gradient)


def solution(mesh):
    placed = (
        P("dom", None),
        P("dom", None),
        P("dom"),
        P("dom", "rep", None, None, None),
        P("dom", "rep", None),
        P("dom", "rep", None),
        P("dom", "rep"),
        P("dom", None, None),
        P("dom", None),
    )
    return jax.shard_map(
        body,
        mesh=mesh,
        in_specs=placed,
        out_specs=(P(("dom", "rep"), None), P(("dom", "rep"), None)),
        check_vma=False,
    )
```

profile of v0, /device:TPU:1, one launch (start us, length us, event | category | flops | bytes accessed | tf_op | source)
XLA Modules:
  0.0 281.2 jit_solution(11773690477429332172)
XLA Ops:
  8.0 0.0 copy-start
  8.0 0.8 convert_rsqrt_fusion
  8.8 0.7 compare_select_fusion
  9.5 0.1 copy.16
  9.6 0.1 reshape.160
  9.7 1.2 multiply_convert_fusion
  10.9 0.0 copy-start.4
  10.9 8.0 %gather_fusion = bf16[2048,128]{1,0:T(8,128)(2,1)} fusion(bf16[1024,128]{1,0:T(8,128)(2,1)S(1)} %get-tuple-element.3, s32[2048]{0:T(1024)S(1)} %broadcast_clamp_fusion), kind=kCustom, calls=%fused_computation | custom fusion | bytes 1056768 | tf_op jit(solution)/shard_map/gather | solution.py:28
  19.0 18.9 %all-to-all-start = ((bf16[128,16,128]{2,1,0:T(8,128)(2,1)}), bf16[128,16,128]{2,1,0:T(8,128)(2,1)}, u32[]{:S(2)}, u32[]{:S(2)}) async-start(bf16[128,16,128]{2,1,0:T(8,128)(2,1)} %bitcast.3), calls=%async_computation | async-start | bytes 1048576 | tf_op jit(solution)/shard_map/all_to_all | solution.py:28
  37.8 0.0 all-reduce.3.cloned.1.call-start
  37.9 0.0 copy-done.4
  38.6 0.7 gather_fusion.3
  39.3 0.0 copy-done
  39.3 1.9 convolution_bitcast_fusion
  41.2 1.9 copy.20
  43.1 0.0 copy-done.3
  43.1 3.0 %fusion = f32[28,16384]{1,0:T(8,128)S(1)} fusion(f32[4,8,128,128]{3,2,1,0:T(8,128)S(1)} %bitcast.47, f32[32]{0:T(128)S(1)} %compare_convert_fusion, s32[32]{0:T(128)S(1)} %bitcast.53), kind=kOutput, calls=%fused_computation.6 | convolution fusion | flops 176162560 | bytes 3932416 | tf_op jit(solution)/shard_map/dot_general | solution.py:62
  46.2 1.3 copy-done.2
  47.5 0.0 slice-start
  47.5 0.9 slice.20
  48.4 0.0 all-reduce.3.cloned.1.call-update
  48.5 0.0 copy-start.5
  48.5 0.4 slice-done
  48.8 1.1 reshape.157
  50.0 0.6 gather_fusion.1
  50.5 51.5 %all-gather.1 = bf16[128,4,128]{2,1,0:T(4,128)(2,1)S(1)} all-gather(bf16[1,4,128]{2,1,0:T(4,128)(2,1)S(1)} %bitcast.52), channel_id=2, replica_groups=mesh['dom'=128,'rep'=4] {'dom'}, dimensions={0}, use_global_device_ids=true | all-gather | bytes 132096 | tf_op jit(solution)/shard_map/all_gather | solution.py:29
  102.0 0.0 all-to-all-done
  102.1 10.2 %all-to-all-start.1 = ((f32[128,16,128]{2,1,0:T(8,128)}), f32[128,16,128]{2,1,0:T(8,128)}, u32[]{:S(2)}, u32[]{:S(2)}) async-start(f32[128,16,128]{2,1,0:T(8,128)} %reshape.157), calls=%async_computation.2 | async-start | bytes 2097152 | tf_op jit(solution)/shard_map/all_to_all | solution.py:72
  112.2 0.2 reduce-scatter.3.cloned.1.call-start
  112.5 1.1 pad_maximum_fusion
  113.6 0.7 gather_fusion.2
  114.3 2.2 convolution_bitcast_fusion.1
  116.5 1.9 copy.18
  118.5 3.0 %fusion.3 = f32[8,16384]{1,0:T(8,128)} fusion(f32[4,8,128,128]{3,2,1,0:T(8,128)S(1)} %bitcast.48, f32[32]{0:T(128)S(1)} %compare_convert_fusion, s32[32]{0:T(128)S(1)} %bitcast.54), kind=kOutput, calls=%fused_computation.9 | convolution fusion | flops 50332160 | bytes 2621696 | tf_op jit(solution)/shard_map/dot_general | solution.py:46
  121.5 2.0 reshape.154
  123.5 0.0 reduce-scatter.3.cloned.1.call-update
  123.5 0.0 reduce-scatter.5.cloned.1.call-start
  123.6 0.1 slice.17
  123.7 1.3 dynamic-slice
  125.6 17.5 %all-to-all-done.1 = f32[128,16,128]{2,1,0:T(8,128)} async-done(((f32[128,16,128]{2,1,0:T(8,128)}), f32[128,16,128]{2,1,0:T(8,128)}, u32[]{:S(2)}, u32[]{:S(2)}) %all-to-all-start.1) | async-done | bytes 1048608 | tf_op jit(solution)/shard_map/all_to_all | solution.py:72
  143.1 12.0 %scatter_fusion = f32[1024,128]{1,0:T(8,128)S(1)} fusion(f32[1024,128]{1,0:T(8,128)S(1)} %slice.17, s32[2048]{0:T(1024)S(1)} %reshape.160, f32[2048,128]{1,0:T(8,128)} %bitcast.19), kind=kCustom, calls=%fused_computation.4 | custom fusion | flops 262144 | bytes 3153920 | tf_op jit(solution)/shard_map/scatter-add | solution.py:73
  155.2 92.6 %all-reduce.3.cloned.1.call-done = f32[512,128]{1,0:T(8,128)} async-done(((f32[512,128]{1,0:T(8,128)}), f32[512,128]{1,0:T(8,128)}) %all-reduce.3.cloned.1.call-update) | async-done | bytes 262160
  247.8 1.0 scatter_custom_fusion.1
  248.8 0.8 copy-done.1
  249.6 0.0 reduce-scatter.5.cloned.1.call-update
  249.6 0.1 dynamic_slice.3
  249.7 22.4 %reduce-scatter.5.cloned.1.call-done = f32[256,128]{1,0:T(8,128)} async-done(((f32[1024,128]{1,0:T(8,128)}), f32[256,128]{1,0:T(8,128)}) %reduce-scatter.5.cloned.1.call-update) | async-done | bytes 131088 | tf_op jit(solution)/shard_map/reduce_scatter | solution.py:78
  272.1 1.7 multiply_convert_fusion.2
  (16 shorter events, 0.1 us)
Async XLA Ops:
  8.0 31.3 %copy-start = (bf16[1,1,32,128,128]{4,3,2,1,0:T(8,128)(2,1)S(1)}, bf16[1,1,32,128,128]{4,3,2,1,0:T(8,128)(2,1)}, u32[]{:S(2)}) copy-start(bf16[1,1,32,128,128]{4,3,2,1,0:T(8,128)(2,1)} %param.12) | copy-start | bytes 3145732
  10.9 27.0 %copy-start.4 = (s32[1,1,32]{2,1,0:T(1,128)S(1)}, s32[1,1,32]{2,1,0:T(1,128)}, u32[]{:S(2)}) copy-start(s32[1,1,32]{2,1,0:T(1,128)} %param.13) | copy-start | bytes 388
  19.0 83.1 %all-to-all-start = ((bf16[128,16,128]{2,1,0:T(8,128)(2,1)}), bf16[128,16,128]{2,1,0:T(8,128)(2,1)}, u32[]{:S(2)}, u32[]{:S(2)}) async-start(bf16[128,16,128]{2,1,0:T(8,128)(2,1)} %bitcast.3), calls=%async_computation | async-start | bytes 1048576 | tf_op jit(solution)/shard_map/all_to_all | solution.py:28
  37.8 210.0 %all-reduce.3.cloned.1.call-start = ((), (), s32[]{:S(2)}) async-start(), calls=%async_computation.6 | async-start | bytes 524288
  41.2 1.9 copy-start.3
  46.2 1.3 copy-start.2
  47.5 1.3 slice-start
  48.5 1.5 copy-start.5
  102.1 41.1 %all-to-all-start.1 = ((f32[128,16,128]{2,1,0:T(8,128)}), f32[128,16,128]{2,1,0:T(8,128)}, u32[]{:S(2)}, u32[]{:S(2)}) async-start(f32[128,16,128]{2,1,0:T(8,128)} %reshape.157), calls=%async_computation.2 | async-start | bytes 2097152 | tf_op jit(solution)/shard_map/all_to_all | solution.py:72
  112.2 137.5 %reduce-scatter.3.cloned.1.call-start = ((), (), s32[]{:S(2)}) async-start(), calls=%async_computation.4 | async-start | bytes 655360 | tf_op jit(solution)/shard_map/reduce_scatter | solution.py:77
  121.5 2.1 slice-start.1
  123.5 148.6 %reduce-scatter.5.cloned.1.call-start = ((), (), s32[]{:S(2)}) async-start(), calls=%async_computation.5 | async-start | bytes 655360 | tf_op jit(solution)/shard_map/reduce_scatter | solution.py:78
  248.8 0.8 copy-start.1
Sparse Core Ops, SparseCore 0:
  48.6 199.1 all-reduce.2
Sparse Core Ops, SparseCore 1:
  123.6 25.4 reduce-scatter.2
  249.7 22.3 reduce-scatter.4
where the time goes:
time: 283 us; the launch traced here: 281 us
  waiting for transfers between devices  133 us (47%)
  blocking collectives  51.5 us (18%)
  starting transfers between devices  29.3 us (10%)
  local copies, waits for them, and re-layouts  22.1 us (8%)
  other arithmetic  18.6 us (7%)
  between operations  17 us (6%)
  matrix products  10.1 us (4%)
    unnamed x4, waiting for transfers between devices  92.7 us
    all_gather x1, blocking collectives, body(): hub_block = lax.all_gather(scaled[hub_rows[0]], 'dom', axis=0, tiled=True)  51.5 us
    reduce_scatter x1, waiting for transfers between devices, body(): lax.psum_scatter(gradient_part, 'rep', scatter_dimension=0, tiled=True)  22.4 us
    all_to_all x1, starting transfers between devices, body(): lax.all_to_all(scaled[send_rows[0]], 'dom', split_axis=0, concat_axis=0,...  18.9 us
    all_to_all x1, waiting for transfers between devices, body(): lax.all_to_all(boundary_part, 'dom', split_axis=0, concat_axis=0, tiled=T...  17.5 us
    scatter-add x1, other arithmetic, body(): gradient_part = local_part.at[send_rows[0]].add(returned)  12 us
    all_to_all x1, starting transfers between devices, body(): lax.all_to_all(boundary_part, 'dom', split_axis=0, concat_axis=0, tiled=T...  10.2 us
    gather x1, local copies, waits for them, and re-layouts, body(): scaled[send_rows[0]]  8.02 us
  transfers between devices with their start and end apart: 5, of which 3 were waited for; matrix products, arithmetic and copies ran while one was open for 13% of the time, Pallas kernels for 0%

commit v1 on v0

v1 whole, which is shorter than its diff:
```python
import jax
import jax.numpy as jnp
from jax import lax
from jax.experimental import pallas as pl
from jax.experimental.pallas import tpu as pltpu
from jax.sharding import PartitionSpec as P

TB = 128
GROUP = 4


def _column(row):
    return jnp.broadcast_to(row, (TB, TB)).T


def _tile_loop(live, step):
    def group(g, carry):
        step(g * GROUP)
        return carry

    lax.fori_loop(0, (live + GROUP - 1) // GROUP, group, 0)


def _before_kernel(live_ref, target_ref, source_ref, hub_ref, degrees_ref, rows_ref, embedding_ref,
                   cotangent_ref, tiles_ref, send_ref, local_ref, scaled_ref, weighted_ref, slots_ref):
    f32, bf16 = jnp.float32, jnp.bfloat16
    own_blocks = degrees_ref.shape[0]
    half = own_blocks // 2
    bound_blocks = rows_ref.shape[0]
    root = lax.rsqrt(degrees_ref[...].astype(f32))
    for b in range(own_blocks):
        part = slice(b * TB, (b + 1) * TB)
        column = _column(root[b:b + 1])
        scaled_ref[part] = (column * embedding_ref[part].astype(f32)).astype(bf16)
        weighted_ref[part] = (column * cotangent_ref[part].astype(f32)).astype(bf16)

    halves = jnp.concatenate([scaled_ref[:half * TB], scaled_ref[half * TB:]], axis=1)
    lane = lax.broadcasted_iota(jnp.int32, (TB, TB), 1)

    def pick(index, count):
        high = index >= half * TB
        low = jnp.where(high, index - half * TB, index)
        onehot = jnp.concatenate(
            [(low == lane[:count] + j * TB).astype(f32).astype(bf16) for j in range(half)], axis=1)
        both = jnp.dot(onehot, halves, preferred_element_type=f32)
        return jnp.where(high, both[:, TB:], both[:, :TB])

    for i in range(bound_blocks):
        index = _column(rows_ref[i:i + 1].astype(f32)).astype(jnp.int32)
        send_ref[8 * i:8 * i + 8, 0:16, :] = pick(index, TB).astype(bf16).reshape(8, 16, TB)
    sub = lax.broadcasted_iota(jnp.int32, (16, TB), 0)
    index = jnp.zeros((16, TB), jnp.int32)
    for j in range(4):
        index = jnp.where(sub == j, hub_ref[j], index)
    hub = pick(index, 16)[:8]

    slots_ref[...] = jnp.zeros(slots_ref.shape, f32)
    live = live_ref[0]

    def step(t):
        products = []
        for k in range(GROUP):
            target = target_ref[t + k]
            w = weighted_ref[pl.ds(pl.multiple_of(target * TB, TB), TB), :]
            products.append(lax.dot_general(
                tiles_ref[t + k], w, (((0,), (0,)), ((), ())), preferred_element_type=f32))
        for k in range(GROUP):
            slots_ref[source_ref[t + k]] += jnp.where(t + k < live, products[k], 0.0)

    _tile_loop(live, step)
    local_ref[...] = slots_ref[:own_blocks].reshape(own_blocks * TB, TB)
    for i in range(bound_blocks):
        send_ref[8 * i:8 * i + 8, 16:32, :] = slots_ref[own_blocks + i].astype(bf16).reshape(8, 16, TB)
    first = lax.broadcasted_iota(jnp.int32, (16, 8, TB), 1) < 4
    hub_tile = jnp.broadcast_to(hub[None], (16, 8, TB))
    for h in range(slots_ref.shape[0] - own_blocks - bound_blocks):
        x = slots_ref[own_blocks + bound_blocks + h].reshape(16, 8, TB)
        odd = jnp.where(first, hub_tile, x)
        even = jnp.where(first, hub_tile, pltpu.roll(x, 4, 1))
        pair = jnp.stack([even, odd], axis=1).reshape(32, 8, TB)
        send_ref[32 * h:32 * h + 32, 32:40, :] = pair.astype(bf16)


def _after_kernel(live_ref, target_ref, source_ref, hub_ref, degrees_ref, rows_ref, arrived_ref, local_ref,
                  scaled_ref, tiles_ref, out_ref, source_rows_ref, forward_ref, gradient_ref):
    f32, bf16 = jnp.float32, jnp.bfloat16
    own_blocks = degrees_ref.shape[0]
    bound_blocks = rows_ref.shape[0]
    for b in range(own_blocks):
        source_rows_ref[b] = scaled_ref[b * TB:(b + 1) * TB]
    for i in range(bound_blocks):
        source_rows_ref[own_blocks + i] = arrived_ref[8 * i:8 * i + 8, 0:16, :].reshape(TB, TB)
    first = lax.broadcasted_iota(jnp.int32, (16, 8, TB), 1) < 4
    hub_total = jnp.zeros((8, TB), f32)
    for h in range(source_rows_ref.shape[0] - own_blocks - bound_blocks):
        x = arrived_ref[32 * h:32 * h + 32, 32:40, :].astype(f32)
        hub_total = hub_total + jnp.sum(x, axis=0)
        x = x.reshape(16, 2, 8, TB)
        merged = jnp.where(first, x[:, 0], pltpu.roll(x[:, 1], 4, 1))
        source_rows_ref[own_blocks + bound_blocks + h] = merged.reshape(TB, TB).astype(bf16)

    forward_ref[...] = jnp.zeros(forward_ref.shape, f32)
    live = live_ref[0]

    def step(t):
        products = [
            jnp.dot(tiles_ref[t + k], source_rows_ref[source_ref[t + k]], preferred_element_type=f32)
            for k in range(GROUP)
        ]
        for k in range(GROUP):
            forward_ref[target_ref[t + k]] += jnp.where(t + k < live, products[k], 0.0)

    _tile_loop(live, step)

    returned = arrived_ref[:, 16:32, :].reshape(bound_blocks * TB, TB)
    sub = lax.broadcasted_iota(jnp.int32, (TB, TB), 0)
    for b in range(own_blocks):
        onehot = jnp.concatenate(
            [(jnp.broadcast_to(rows_ref[i:i + 1], (TB, TB)) == sub + b * TB).astype(f32).astype(bf16)
             for i in range(bound_blocks)], axis=1)
        part = slice(b * TB, (b + 1) * TB)
        gradient_ref[part] = local_ref[part] + jnp.dot(onehot, returned, preferred_element_type=f32)
    for j in range(4):
        row = pl.ds(hub_ref[j], 1)
        gradient_ref[row, :] = gradient_ref[row, :] + hub_total[4 + j:5 + j]

    root = lax.rsqrt(degrees_ref[...].astype(f32))
    replicas = out_ref.shape[0]
    each = own_blocks // replicas
    for b in range(own_blocks):
        column = _column(root[b:b + 1])
        c, at = b // each, (b % each) * TB
        out_ref[c, at:at + TB] = (column * forward_ref[b]).astype(bf16)
        at += each * TB
        out_ref[c, at:at + TB] = (column * gradient_ref[b * TB:(b + 1) * TB]).astype(bf16)


def body(embedding, cotangent, degrees, tile_values, tile_target, tile_source, live_tile_count, send_rows, hub_rows):
    f32, bf16 = jnp.float32, jnp.bfloat16
    own_rows, width = embedding.shape
    slots = tile_values.shape[2]
    partitions, pair_rows = send_rows.shape[1:]
    hubs = hub_rows.shape[1]
    replicas = lax.axis_size("rep")
    own_blocks = own_rows // TB
    source_blocks = (own_rows + partitions * (pair_rows + hubs)) // TB
    tiles = tile_values.reshape(slots, TB, TB)
    small = (live_tile_count.reshape(1), tile_target.reshape(slots), tile_source.reshape(slots), hub_rows.reshape(hubs))
    degree_blocks = degrees.reshape(own_blocks, TB)
    rows = send_rows.reshape(partitions * pair_rows // TB, TB)
    in_smem = pl.BlockSpec(memory_space=pltpu.SMEM)
    in_vmem = pl.BlockSpec(memory_space=pltpu.VMEM)
    pair = 2 * (pair_rows + hubs)

    send, local, scaled = pl.pallas_call(
        _before_kernel,
        out_shape=(
            jax.ShapeDtypeStruct((partitions, pair, width), bf16),
            jax.ShapeDtypeStruct((own_rows, width), f32),
            jax.ShapeDtypeStruct((own_rows, width), bf16),
        ),
        in_specs=[in_smem] * 4 + [in_vmem] * 5,
        out_specs=(in_vmem,) * 3,
        scratch_shapes=[pltpu.VMEM((own_rows, width), bf16), pltpu.VMEM((source_blocks, TB, width), f32)],
        name="before",
    )(*small, degree_blocks, rows, embedding, cotangent, tiles)

    arrived = lax.all_to_all(send, "dom", split_axis=0, concat_axis=0, tiled=True)

    exchange = pl.pallas_call(
        _after_kernel,
        out_shape=jax.ShapeDtypeStruct((replicas, 2 * own_rows // replicas, width), bf16),
        in_specs=[in_smem] * 4 + [in_vmem] * 6,
        out_specs=in_vmem,
        scratch_shapes=[
            pltpu.VMEM((source_blocks, TB, width), bf16),
            pltpu.VMEM((own_blocks, TB, width), f32),
            pltpu.VMEM((own_rows, width), f32),
        ],
        name="after",
    )(*small, degree_blocks, rows, arrived, local, scaled, tiles)

    parts = lax.all_to_all(exchange, "rep", split_axis=0, concat_axis=0, tiled=True)
    total = jnp.sum(parts.astype(f32), axis=0).astype(bf16)
    out_rows = own_rows // replicas
    return total[:out_rows], total[out_rows:]


def solution(mesh):
    placed = (
        P("dom", None),
        P("dom", None),
        P("dom"),
        P("dom", "rep", None, None, None),
        P("dom", "rep", None),
        P("dom", "rep", None),
        P("dom", "rep"),
        P("dom", None, None),
        P("dom", None),
    )
    return jax.shard_map(
        body,
        mesh=mesh,
        in_specs=placed,
        out_specs=(P(("dom", "rep"), None), P(("dom", "rep"), None)),
        check_vma=False,
    )
```

time: 283 us -> 81.3 us (0.29)
  waiting for transfers between devices: 133 us -> 0 us
  starting transfers between devices: 29.3 us -> 0 us
  local copies, waits for them, and re-layouts: 22.1 us -> 2.14 us
  other arithmetic: 18.6 us -> 0.08 us
  blocking collectives: 51.5 us -> 68.4 us
  between operations: 17 us -> 1.28 us
  matrix products: 10.1 us -> 0 us
  Pallas kernels: 0 us -> 8.62 us
    unnamed x4 -> x0, waiting for transfers between devices: 92.7 us -> none
    all_to_all x0 -> x2, blocking collectives: none -> 68.4 us  [the longest x1 55.2 us: body(): lax.all_to_all(send, 'dom', split_axis=0, concat_axis=0, tiled=True)]
    all_gather x1 -> x0, blocking collectives: 51.5 us -> none  [body(): hub_block = lax.all_gather(scaled[hub_rows[0]], 'dom', axis=0, tiled=True)]
    all_to_all x2 -> x0, starting transfers between devices: 29 us -> none  [the longest x1 18.9 us: body(): lax.all_to_all(scaled[send_rows[0]], 'dom', split_axis=0, concat_axis=0,...]
    reduce_scatter x2 -> x0, waiting for transfers between devices: 22.4 us -> none  [the longest x1 22.4 us: body(): lax.psum_scatter(gradient_part, 'rep', scatter_dimension=0, tiled=True)]
    all_to_all x2 -> x0, waiting for transfers between devices: 17.5 us -> none  [the longest x1 17.5 us: body(): lax.all_to_all(boundary_part, 'dom', split_axis=0, concat_axis=0, tiled=T...]
    scatter-add x2 -> x0, other arithmetic: 13 us -> none  [the longest x1 12 us: body(): gradient_part = local_part.at[send_rows[0]].add(returned)]
    dot_general x4 -> x0, matrix products: 10.1 us -> none  [the longest x1 3.03 us: body(): jnp.dot(target_onehot, message_product.reshape(slot_grand_total, -1), pre...]
  transfers between devices with their start and end apart: 5 -> 0, of which waited for: 3 -> 0; matrix products, arithmetic and copies ran while one was open for 13% -> 0% of each run, Pallas kernels for 0% -> 0%
where the time goes in v1:
time: 81.3 us; the launch traced here: 80.5 us
  blocking collectives  68.4 us (84%)
  Pallas kernels  8.62 us (11%)
  local copies, waits for them, and re-layouts  2.14 us (3%)
  between operations  1.28 us (2%)
    all_to_all x1, blocking collectives, body(): lax.all_to_all(send, 'dom', split_axis=0, concat_axis=0, tiled=True)  55.2 us
    all_to_all x1, blocking collectives, body(): lax.all_to_all(exchange, 'rep', split_axis=0, concat_axis=0, tiled=True)  13.1 us
    pallas_call x1, Pallas kernels, body(): pl.pallas_call(_after_kernel, out_shape=jax.ShapeDtypeStruct((replicas, 2...  4.37 us
    pallas_call x1, Pallas kernels, body(): pl.pallas_call(_before_kernel, out_shape=(jax.ShapeDtypeStruct((partition...  4.25 us

profile of v1, /device:TPU:1, one launch (start us, length us, event | category | flops | bytes accessed | tf_op | source)
XLA Modules:
  0.0 80.5 jit_solution(2377383206427985797)
XLA Ops:
  1.3 0.8 copy.12
  2.1 0.7 reshape.30.rows_ref
  2.8 4.3 %before.1 = (bf16[128,40,128]{2,1,0:T(8,128)(2,1)}, f32[1024,128]{1,0:T(8,128)}, bf16[1024,128]{1,0:T(8,128)(2,1)}) custom-call(s32[1]{0:T(128)} %bitcast.6.live_ref, s32[32]{0:T(128)} %bitcast.12, s32[32]{0:T(128)} %bitcast.14, s32[4]{0:T(128)} %bitcast.16, s32[8,128]{1,0:T(8,128)} %bitcast.10, s32[16,128]{1,0:T(8,128)} %reshape.30.rows_ref, ...), custom_call_target="tpu_custom_call" | custom-call | tf_op jit(solution)/shard_map/before/pallas_call | solution.py:155
  7.0 55.2 %all_to_all.10.arrived_ref = bf16[128,40,128]{2,1,0:T(8,128)(2,1)} all-to-all(bf16[128,40,128]{2,1,0:T(8,128)(2,1)} %get-tuple-element.5), channel_id=1, replica_groups=mesh['dom'=128,'rep'=4] {'dom'}, dimensions={0} | all-to-all | bytes 2621440 | tf_op jit(solution)/shard_map/all_to_all | solution.py:168
  62.2 4.4 %after.1 = bf16[4,512,128]{2,1,0:T(8,128)(2,1)} custom-call(s32[1]{0:T(128)} %bitcast.7.live_ref, s32[32]{0:T(128)} %bitcast.13, s32[32]{0:T(128)} %bitcast.15, s32[4]{0:T(128)} %bitcast.17, s32[8,128]{1,0:T(8,128)} %bitcast.11, s32[16,128]{1,0:T(8,128)} %reshape.30.rows_ref, bf16[128,40,128]{2,1,0:T(8,128)(2,1)} %all_to_all.10.arrived_ref, ...), custom_call_target="tpu_custom_call" | custom-call | tf_op jit(solution)/shard_map/after/pallas_call | solution.py:170
  66.6 13.1 %all_to_all.11 = bf16[4,512,128]{2,1,0:T(8,128)(2,1)S(1)} all-to-all(bf16[4,512,128]{2,1,0:T(8,128)(2,1)} %after.1), channel_id=1, replica_groups=mesh['dom'=128,'rep'=4] {'rep'}, dimensions={0} | all-to-all | bytes 1048576 | tf_op jit(solution)/shard_map/all_to_all | solution.py:183
  79.7 0.1 reduce_sum.12
  79.8 0.7 fusion

commit v2 on v1

v2 whole, which is shorter than its diff:
```python
import jax
import jax.numpy as jnp
from jax import lax
from jax.experimental import pallas as pl
from jax.experimental.pallas import tpu as pltpu
from jax.sharding import PartitionSpec as P

TB = 128
GROUP = 4


def _column(row):
    return jnp.broadcast_to(row, (TB, TB)).T


def _tile_loop(live, step):
    def group(g, carry):
        step(g * GROUP)
        return carry

    lax.fori_loop(0, (live + GROUP - 1) // GROUP, group, 0)


def _gather_kernel(hub_ref, degrees_ref, rows_ref, embedding_ref, send_ref, scaled_ref, hub_rows_ref, order_ref):
    f32, bf16 = jnp.float32, jnp.bfloat16
    own_blocks = degrees_ref.shape[0]
    half = own_blocks // 2
    pair_rows = rows_ref.shape[0]
    root = lax.rsqrt(degrees_ref[...].astype(f32))
    for b in range(own_blocks):
        part = slice(b * TB, (b + 1) * TB)
        scaled_ref[part] = (_column(root[b:b + 1]) * embedding_ref[part].astype(f32)).astype(bf16)

    halves = jnp.concatenate([scaled_ref[:half * TB], scaled_ref[half * TB:]], axis=1)
    lane = lax.broadcasted_iota(jnp.int32, (TB, TB), 1)

    def pick(index, count):
        high = index >= half * TB
        low = jnp.where(high, index - half * TB, index)
        onehot = jnp.concatenate(
            [(low == lane[:count] + j * TB).astype(f32).astype(bf16) for j in range(half)], axis=1)
        both = jnp.dot(onehot, halves, preferred_element_type=f32)
        return jnp.where(high, both[:, TB:], both[:, :TB])

    for k in range(pair_rows):
        index = _column(rows_ref[k:k + 1].astype(f32)).astype(jnp.int32)
        order_ref[pl.ds(k, TB, stride=pair_rows), :] = pick(index, TB)
    send_ref[...] = order_ref[...].astype(bf16).reshape(send_ref.shape)
    sub = lax.broadcasted_iota(jnp.int32, (16, TB), 0)
    index = jnp.zeros((16, TB), jnp.int32)
    for j in range(4):
        index = jnp.where(sub == j, hub_ref[j], index)
    hub_rows_ref[...] = pick(index, 16)[:8]


def _backward_kernel(live_ref, target_ref, source_ref, degrees_ref, cotangent_ref, hub_rows_ref, tiles_ref,
                     send_ref, local_ref, weighted_ref, slots_ref):
    f32, bf16 = jnp.float32, jnp.bfloat16
    own_blocks = degrees_ref.shape[0]
    bound_blocks = send_ref.shape[0] // 8
    root = lax.rsqrt(degrees_ref[...].astype(f32))
    for b in range(own_blocks):
        part = slice(b * TB, (b + 1) * TB)
        weighted_ref[part] = (_column(root[b:b + 1]) * cotangent_ref[part].astype(f32)).astype(bf16)
    slots_ref[...] = jnp.zeros(slots_ref.shape, f32)
    live = live_ref[0]

    def step(t):
        products = []
        for k in range(GROUP):
            target = target_ref[t + k]
            w = weighted_ref[pl.ds(pl.multiple_of(target * TB, TB), TB), :]
            products.append(lax.dot_general(
                tiles_ref[t + k], w, (((0,), (0,)), ((), ())), preferred_element_type=f32))
        for k in range(GROUP):
            slots_ref[source_ref[t + k]] += jnp.where(t + k < live, products[k], 0.0)

    _tile_loop(live, step)
    local_ref[...] = slots_ref[:own_blocks].reshape(own_blocks * TB, TB)
    for i in range(bound_blocks):
        send_ref[8 * i:8 * i + 8, 0:16, :] = slots_ref[own_blocks + i].astype(bf16).reshape(8, 16, TB)
    first = lax.broadcasted_iota(jnp.int32, (16, 8, TB), 1) < 4
    hub_tile = jnp.broadcast_to(hub_rows_ref[...][None], (16, 8, TB))
    for h in range(slots_ref.shape[0] - own_blocks - bound_blocks):
        x = slots_ref[own_blocks + bound_blocks + h].reshape(16, 8, TB)
        odd = jnp.where(first, hub_tile, x)
        even = jnp.where(first, hub_tile, pltpu.roll(x, 4, 1))
        pair = jnp.stack([even, odd], axis=1).reshape(32, 8, TB)
        send_ref[32 * h:32 * h + 32, 16:24, :] = pair.astype(bf16)


def _forward_kernel(live_ref, target_ref, source_ref, arrived_ref, scaled_ref, tiles_ref, forward_ref, source_rows_ref):
    f32 = jnp.float32
    own_blocks = forward_ref.shape[0]
    bound_blocks = arrived_ref.shape[0] // 8
    for b in range(own_blocks):
        source_rows_ref[b] = scaled_ref[b * TB:(b + 1) * TB]
    for i in range(bound_blocks):
        source_rows_ref[own_blocks + i] = arrived_ref[8 * i:8 * i + 8].reshape(TB, TB)
    forward_ref[...] = jnp.zeros(forward_ref.shape, f32)
    live = live_ref[0]
    here = own_blocks + bound_blocks

    def step(t):
        products = [
            jnp.dot(tiles_ref[t + k], source_rows_ref[jnp.minimum(source_ref[t + k], here - 1)],
                    preferred_element_type=f32) for k in range(GROUP)
        ]
        for k in range(GROUP):
            use = jnp.logical_and(t + k < live, source_ref[t + k] < here)
            forward_ref[target_ref[t + k]] += jnp.where(use, products[k], 0.0)

    _tile_loop(live, step)


def _finish_kernel(live_ref, target_ref, source_ref, hub_ref, degrees_ref, rows_ref, arrived_ref, local_ref,
                   early_ref, tiles_ref, out_ref, source_rows_ref, forward_ref, gradient_ref):
    f32, bf16 = jnp.float32, jnp.bfloat16
    own_blocks = degrees_ref.shape[0]
    bound_blocks = rows_ref.shape[0]
    first = lax.broadcasted_iota(jnp.int32, (16, 8, TB), 1) < 4
    hub_total = jnp.zeros((8, TB), f32)
    for h in range(source_rows_ref.shape[0]):
        x = arrived_ref[32 * h:32 * h + 32, 16:24, :].astype(f32)
        hub_total = hub_total + jnp.sum(x, axis=0)
        x = x.reshape(16, 2, 8, TB)
        merged = jnp.where(first, x[:, 0], pltpu.roll(x[:, 1], 4, 1))
        source_rows_ref[h] = merged.reshape(TB, TB).astype(bf16)
    forward_ref[...] = early_ref[...]
    here = own_blocks + bound_blocks

    def slot(t, carry):
        @pl.when(source_ref[t] >= here)
        def _():
            forward_ref[target_ref[t]] += jnp.dot(
                tiles_ref[t], source_rows_ref[source_ref[t] - here], preferred_element_type=f32)
        return carry

    lax.fori_loop(0, live_ref[0], slot, 0)

    returned = arrived_ref[:, 0:16, :].reshape(bound_blocks * TB, TB)
    sub = lax.broadcasted_iota(jnp.int32, (TB, TB), 0)
    for b in range(own_blocks):
        onehot = jnp.concatenate(
            [(jnp.broadcast_to(rows_ref[i:i + 1], (TB, TB)) == sub + b * TB).astype(f32).astype(bf16)
             for i in range(bound_blocks)], axis=1)
        part = slice(b * TB, (b + 1) * TB)
        gradient_ref[part] = local_ref[part] + jnp.dot(onehot, returned, preferred_element_type=f32)
    for j in range(4):
        row = pl.ds(hub_ref[j], 1)
        gradient_ref[row, :] = gradient_ref[row, :] + hub_total[4 + j:5 + j]

    root = lax.rsqrt(degrees_ref[...].astype(f32))
    each = own_blocks // out_ref.shape[0]
    for b in range(own_blocks):
        column = _column(root[b:b + 1])
        c, at = b // each, (b % each) * TB
        out_ref[c, at:at + TB] = (column * forward_ref[b]).astype(bf16)
        at += each * TB
        out_ref[c, at:at + TB] = (column * gradient_ref[b * TB:(b + 1) * TB]).astype(bf16)


def body(embedding, cotangent, degrees, tile_values, tile_target, tile_source, live_tile_count, send_rows, hub_rows):
    f32, bf16 = jnp.float32, jnp.bfloat16
    own_rows, width = embedding.shape
    slots = tile_values.shape[2]
    partitions, pair_rows = send_rows.shape[1:]
    hubs = hub_rows.shape[1]
    replicas = lax.axis_size("rep")
    own_blocks = own_rows // TB
    source_blocks = (own_rows + partitions * (pair_rows + hubs)) // TB
    tiles = tile_values.reshape(slots, TB, TB)
    live, target, source, hub = (
        live_tile_count.reshape(1), tile_target.reshape(slots), tile_source.reshape(slots), hub_rows.reshape(hubs))
    degree_blocks = degrees.reshape(own_blocks, TB)
    rows = send_rows.reshape(partitions * pair_rows // TB, TB)
    rows_by_place = send_rows[0].T
    in_smem = pl.BlockSpec(memory_space=pltpu.SMEM)
    in_vmem = pl.BlockSpec(memory_space=pltpu.VMEM)
    shape = jax.ShapeDtypeStruct

    forward_rows, scaled, hub_own = pl.pallas_call(
        _gather_kernel,
        out_shape=(shape((partitions, pair_rows, width), bf16), shape((own_rows, width), bf16), shape((8, width), f32)),
        in_specs=[in_smem] + [in_vmem] * 3,
        out_specs=(in_vmem,) * 3,
        scratch_shapes=[pltpu.VMEM((partitions * pair_rows, width), f32)],
        name="gather",
    )(hub, degree_blocks, rows_by_place, embedding)
    arrived = lax.all_to_all(forward_rows, "dom", split_axis=0, concat_axis=0, tiled=True)

    partials, local = pl.pallas_call(
        _backward_kernel,
        out_shape=(shape((partitions, pair_rows + 2 * hubs, width), bf16), shape((own_rows, width), f32)),
        in_specs=[in_smem] * 3 + [in_vmem] * 4,
        out_specs=(in_vmem,) * 2,
        scratch_shapes=[pltpu.VMEM((own_rows, width), bf16), pltpu.VMEM((source_blocks, TB, width), f32)],
        name="backward",
    )(live, target, source, degree_blocks, cotangent, hub_own, tiles)
    returned = lax.all_to_all(partials, "dom", split_axis=0, concat_axis=0, tiled=True)

    early = pl.pallas_call(
        _forward_kernel,
        out_shape=shape((own_blocks, TB, width), f32),
        in_specs=[in_smem] * 3 + [in_vmem] * 3,
        out_specs=in_vmem,
        scratch_shapes=[pltpu.VMEM((own_blocks + partitions * pair_rows // TB, TB, width), bf16)],
        name="forward",
    )(live, target, source, arrived, scaled, tiles)

    exchange = pl.pallas_call(
        _finish_kernel,
        out_shape=shape((replicas, 2 * own_rows // replicas, width), bf16),
        in_specs=[in_smem] * 4 + [in_vmem] * 6,
        out_specs=in_vmem,
        scratch_shapes=[
            pltpu.VMEM((partitions * hubs // TB, TB, width), bf16),
            pltpu.VMEM((own_blocks, TB, width), f32),
            pltpu.VMEM((own_rows, width), f32),
        ],
        name="finish",
    )(live, target, source, hub, degree_blocks, rows, returned, local, early, tiles)

    parts = lax.all_to_all(exchange, "rep", split_axis=0, concat_axis=0, tiled=True)
    total = jnp.sum(parts.astype(f32), axis=0).astype(bf16)
    out_rows = own_rows // replicas
    return total[:out_rows], total[out_rows:]


def solution(mesh):
    placed = (
        P("dom", None),
        P("dom", None),
        P("dom"),
        P("dom", "rep", None, None, None),
        P("dom", "rep", None),
        P("dom", "rep", None),
        P("dom", "rep"),
        P("dom", None, None),
        P("dom", None),
    )
    return jax.shard_map(
        body,
        mesh=mesh,
        in_specs=placed,
        out_specs=(P(("dom", "rep"), None), P(("dom", "rep"), None)),
        check_vma=False,
    )
```

time: 81.3 us -> 95.2 us (1.17)
  blocking collectives: 68.4 us -> 14.2 us
  waiting for transfers between devices: 0 us -> 39.1 us
  starting transfers between devices: 0 us -> 23.8 us
  Pallas kernels: 8.62 us -> 13.1 us
  local copies, waits for them, and re-layouts: 2.14 us -> 3.13 us
    all_to_all x1 -> x0, blocking collectives: 55.2 us -> none  [body(): lax.all_to_all(send, 'dom', split_axis=0, concat_axis=0, tiled=True)]
    all_to_all x0 -> x2, waiting for transfers between devices: none -> 39.1 us  [the longest x1 22.4 us: body(): lax.all_to_all(partials, 'dom', split_axis=0, concat_axis=0, tiled=True)]
    all_to_all x0 -> x2, starting transfers between devices: none -> 23.8 us  [the longest x1 18.4 us: body(): lax.all_to_all(forward_rows, 'dom', split_axis=0, concat_axis=0, tiled=True)]
    pallas_call x2 -> x4, Pallas kernels: 8.62 us -> 13.1 us  [the longest x1 4.13 us: body(): pl.pallas_call(_finish_kernel, out_shape=shape((replicas, 2 * own_rows //...]
    all_to_all x1, blocking collectives: 13.1 us -> 14.2 us  [body(): lax.all_to_all(exchange, 'rep', split_axis=0, concat_axis=0, tiled=True)]
    unnamed x1 -> x7, local copies, waits for them, and re-layouts: 0.8 us -> 1.79 us
  transfers between devices with their start and end apart: 0 -> 2, of which waited for: 0 -> 2; matrix products, arithmetic and copies ran while one was open for 0% -> 1% of each run, Pallas kernels for 0% -> 6%
where the time goes in v2:
time: 95.2 us; the launch traced here: 94.8 us
  waiting for transfers between devices  39.1 us (41%)
  starting transfers between devices  23.8 us (25%)
  blocking collectives  14.2 us (15%)
  Pallas kernels  13.1 us (14%)
  local copies, waits for them, and re-layouts  3.13 us (3%)
  between operations  1.31 us (1%)
    all_to_all x1, waiting for transfers between devices, body(): lax.all_to_all(partials, 'dom', split_axis=0, concat_axis=0, tiled=True)  22.4 us
    all_to_all x1, starting transfers between devices, body(): lax.all_to_all(forward_rows, 'dom', split_axis=0, concat_axis=0, tiled=True)  18.4 us
    all_to_all x1, waiting for transfers between devices, body(): lax.all_to_all(forward_rows, 'dom', split_axis=0, concat_axis=0, tiled=True)  16.7 us
    all_to_all x1, blocking collectives, body(): lax.all_to_all(exchange, 'rep', split_axis=0, concat_axis=0, tiled=True)  14.2 us
    all_to_all x1, starting transfers between devices, body(): lax.all_to_all(partials, 'dom', split_axis=0, concat_axis=0, tiled=True)  5.4 us
    pallas_call x1, Pallas kernels, body(): pl.pallas_call(_finish_kernel, out_shape=shape((replicas, 2 * own_rows //...  4.13 us
    pallas_call x1, Pallas kernels, body(): pl.pallas_call(_backward_kernel, out_shape=(shape((partitions, pair_rows...  3.19 us
    pallas_call x1, Pallas kernels, body(): pl.pallas_call(_gather_kernel, out_shape=(shape((partitions, pair_rows, w...  3.08 us
  transfers between devices with their start and end apart: 2, of which 2 were waited for; matrix products, arithmetic and copies ran while one was open for 1% of the time, Pallas kernels for 6%

profile of v2, /device:TPU:1, one launch (start us, length us, event | category | flops | bytes accessed | tf_op | source)
XLA Modules:
  0.0 94.8 jit_solution(9802073378030061725)
XLA Ops:
  0.6 3.1 %gather.1 = (bf16[128,16,128]{2,1,0:T(8,128)(2,1)}, bf16[1024,128]{1,0:T(8,128)(2,1)}, f32[8,128]{1,0:T(8,128)}) custom-call(s32[4]{0:T(128)} %bitcast.25, s32[8,128]{1,0:T(8,128)} %bitcast.15, s32[16,128]{1,0:T(8,128)} %bitcast.18, bf16[1024,128]{1,0:T(8,128)(2,1)} %embedding_ref.1), custom_call_target="tpu_custom_call" | custom-call | tf_op jit(solution)/shard_map/gather/pallas_call | solution.py:182
  3.7 18.4 %all-to-all-start.1 = ((bf16[128,16,128]{2,1,0:T(8,128)(2,1)}), bf16[128,16,128]{2,1,0:T(8,128)(2,1)S(1)}, u32[]{:S(2)}, u32[]{:S(2)}) async-start(bf16[128,16,128]{2,1,0:T(8,128)(2,1)} %get-tuple-element.10), calls=%async_computation.1 | async-start | bytes 1048576 | tf_op jit(solution)/shard_map/all_to_all | solution.py:190
  22.8 3.2 %backward.1 = (bf16[128,24,128]{2,1,0:T(8,128)(2,1)}, f32[1024,128]{1,0:T(8,128)}) custom-call(s32[1]{0:T(128)} %bitcast.9.live_ref, s32[32]{0:T(128)} %bitcast.19, s32[32]{0:T(128)} %bitcast.22, s32[8,128]{1,0:T(8,128)} %bitcast.16, bf16[1024,128]{1,0:T(8,128)(2,1)} %cotangent_ref.1, f32[8,128]{1,0:T(8,128)} %get-tuple-element.7.hub_rows_ref, ...), custom_call_target="tpu_custom_call" | custom-call | tf_op jit(solution)/shard_map/backward/pallas_call | solution.py:192
  26.0 16.7 %all-to-all-done.1.arrived_ref = bf16[128,16,128]{2,1,0:T(8,128)(2,1)S(1)} async-done(((bf16[128,16,128]{2,1,0:T(8,128)(2,1)}), bf16[128,16,128]{2,1,0:T(8,128)(2,1)S(1)}, u32[]{:S(2)}, u32[]{:S(2)}) %all-to-all-start.1) | async-done | bytes 524320 | tf_op jit(solution)/shard_map/all_to_all | solution.py:190
  42.7 0.0 copy-start.1
  42.7 0.0 copy-start.2
  42.7 0.8 copy-done.1
  43.5 5.4 %all-to-all-start = ((bf16[128,24,128]{2,1,0:T(8,128)(2,1)}), bf16[128,24,128]{2,1,0:T(8,128)(2,1)S(1)}, u32[]{:S(2)}, u32[]{:S(2)}) async-start(bf16[128,24,128]{2,1,0:T(8,128)(2,1)} %get-tuple-element.8), calls=%async_computation | async-start | bytes 1572864 | tf_op jit(solution)/shard_map/all_to_all | solution.py:200
  48.9 0.0 copy-done.2
  48.9 0.1 copy.12
  49.0 0.7 reshape.30.rows_ref
  49.7 2.7 %forward.1.early_ref = f32[8,128,128]{2,1,0:T(8,128)} custom-call(s32[1]{0:T(128)} %bitcast.10.live_ref, s32[32]{0:T(128)} %bitcast.20, s32[32]{0:T(128)} %bitcast.23, bf16[128,16,128]{2,1,0:T(8,128)(2,1)} %copy-done.1, bf16[1024,128]{1,0:T(8,128)(2,1)} %get-tuple-element.11.scaled_ref, bf16[32,128,128]{2,1,0:T(8,128)(2,1)} %bitcast.13), custom_call_target="tpu_custom_call" | custom-call | tf_op jit(solution)/shard_map/forward/pallas_call | solution.py:202
  52.4 22.4 %all-to-all-done.arrived_ref = bf16[128,24,128]{2,1,0:T(8,128)(2,1)S(1)} async-done(((bf16[128,24,128]{2,1,0:T(8,128)(2,1)}), bf16[128,24,128]{2,1,0:T(8,128)(2,1)S(1)}, u32[]{:S(2)}, u32[]{:S(2)}) %all-to-all-start) | async-done | bytes 786464 | tf_op jit(solution)/shard_map/all_to_all | solution.py:200
  74.9 0.0 copy-start
  74.9 0.9 copy-done
  75.7 4.1 %finish.1 = bf16[4,512,128]{2,1,0:T(8,128)(2,1)} custom-call(s32[1]{0:T(128)} %bitcast.11.live_ref, s32[32]{0:T(128)} %bitcast.21, s32[32]{0:T(128)} %bitcast.24, s32[4]{0:T(128)} %bitcast.26, s32[8,128]{1,0:T(8,128)} %bitcast.17, s32[16,128]{1,0:T(8,128)} %reshape.30.rows_ref, bf16[128,24,128]{2,1,0:T(8,128)(2,1)} %copy-done, ...), custom_call_target="tpu_custom_call" | custom-call | tf_op jit(solution)/shard_map/finish/pallas_call | solution.py:211
  79.9 14.2 %all_to_all.15 = bf16[4,512,128]{2,1,0:T(8,128)(2,1)S(1)} all-to-all(bf16[4,512,128]{2,1,0:T(8,128)(2,1)} %finish.1), channel_id=1, replica_groups=mesh['dom'=128,'rep'=4] {'rep'}, dimensions={0} | all-to-all | bytes 1048576 | tf_op jit(solution)/shard_map/all_to_all | solution.py:224
  94.1 0.1 reduce_sum.12
  94.2 0.7 fusion
Async XLA Ops:
  3.7 39.0 %all-to-all-start.1 = ((bf16[128,16,128]{2,1,0:T(8,128)(2,1)}), bf16[128,16,128]{2,1,0:T(8,128)(2,1)S(1)}, u32[]{:S(2)}, u32[]{:S(2)}) async-start(bf16[128,16,128]{2,1,0:T(8,128)(2,1)} %get-tuple-element.10), calls=%async_computation.1 | async-start | bytes 1048576 | tf_op jit(solution)/shard_map/all_to_all | solution.py:190
  42.7 0.8 copy-start.1
  42.7 6.2 %copy-start.2 = (s32[1,128,16]{1,2,0:T(8,128)S(1)}, s32[1,128,16]{1,2,0:T(8,128)}, u32[]{:S(2)}) copy-start(s32[1,128,16]{1,2,0:T(8,128)} %param.16) | copy-start | bytes 24580
  43.5 31.4 %all-to-all-start = ((bf16[128,24,128]{2,1,0:T(8,128)(2,1)}), bf16[128,24,128]{2,1,0:T(8,128)(2,1)S(1)}, u32[]{:S(2)}, u32[]{:S(2)}) async-start(bf16[128,24,128]{2,1,0:T(8,128)(2,1)} %get-tuple-element.8), calls=%async_computation | async-start | bytes 1572864 | tf_op jit(solution)/shard_map/all_to_all | solution.py:200
  74.9 0.9 copy-start

commit v3 on v1

--- a/solution.py
+++ b/solution.py
@@ -21,18 +21,33 @@
     lax.fori_loop(0, (live + GROUP - 1) // GROUP, group, 0)
 
 
-def _before_kernel(live_ref, target_ref, source_ref, hub_ref, degrees_ref, rows_ref, embedding_ref,
-                   cotangent_ref, tiles_ref, send_ref, local_ref, scaled_ref, weighted_ref, slots_ref):
+def _fetch(pairs, sems):
+    copies = [pltpu.make_async_copy(src, dst, sems.at[i]) for i, (src, dst) in enumerate(pairs)]
+    for copy in copies:
+        copy.start()
+    return copies
+
+
+def _before_kernel(live_hbm, target_hbm, source_hbm, hub_hbm, degrees_hbm, rows_hbm, embedding_hbm, cotangent_hbm,
+                   tiles_hbm, send_hbm, local_hbm, scaled_hbm, live_ref, target_ref, source_ref, hub_ref, degrees_ref,
+                   rows_ref, embedding_ref, cotangent_ref, tiles_ref, early_ref, late_ref, scaled_ref, weighted_ref,
+                   slots_ref, order_ref, sems):
     f32, bf16 = jnp.float32, jnp.bfloat16
+    copies = _fetch((
+        (degrees_hbm, degrees_ref), (embedding_hbm, embedding_ref), (rows_hbm, rows_ref), (hub_hbm, hub_ref),
+        (cotangent_hbm, cotangent_ref), (live_hbm, live_ref), (target_hbm, target_ref), (source_hbm, source_ref),
+        (tiles_hbm, tiles_ref)), sems)
     own_blocks = degrees_ref.shape[0]
     half = own_blocks // 2
-    bound_blocks = rows_ref.shape[0]
+    pair_rows = rows_ref.shape[0]
+    bound_blocks = send_hbm.shape[0] // 8
+    slots_ref[...] = jnp.zeros(slots_ref.shape, f32)
+    for copy in copies[:4]:
+        copy.wait()
     root = lax.rsqrt(degrees_ref[...].astype(f32))
     for b in range(own_blocks):
         part = slice(b * TB, (b + 1) * TB)
-        column = _column(root[b:b + 1])
-        scaled_ref[part] = (column * embedding_ref[part].astype(f32)).astype(bf16)
-        weighted_ref[part] = (column * cotangent_ref[part].astype(f32)).astype(bf16)
+        scaled_ref[part] = (_column(root[b:b + 1]) * embedding_ref[part].astype(f32)).astype(bf16)
 
     halves = jnp.concatenate([scaled_ref[:half * TB], scaled_ref[half * TB:]], axis=1)
     lane = lax.broadcasted_iota(jnp.int32, (TB, TB), 1)
@@ -45,16 +60,25 @@
         both = jnp.dot(onehot, halves, preferred_element_type=f32)
         return jnp.where(high, both[:, TB:], both[:, :TB])
 
-    for i in range(bound_blocks):
-        index = _column(rows_ref[i:i + 1].astype(f32)).astype(jnp.int32)
-        send_ref[8 * i:8 * i + 8, 0:16, :] = pick(index, TB).astype(bf16).reshape(8, 16, TB)
+    for k in range(pair_rows):
+        index = _column(rows_ref[k:k + 1].astype(f32)).astype(jnp.int32)
+        order_ref[pl.ds(k, TB, stride=pair_rows), :] = pick(index, TB)
+    early_ref[...] = order_ref[...].astype(bf16).reshape(bound_blocks * 8, 16, TB)
+    out = [pltpu.make_async_copy(early_ref, send_hbm.at[:, 0:16, :], sems.at[9]),
+           pltpu.make_async_copy(scaled_ref, scaled_hbm, sems.at[10])]
+    for copy in out:
+        copy.start()
     sub = lax.broadcasted_iota(jnp.int32, (16, TB), 0)
     index = jnp.zeros((16, TB), jnp.int32)
     for j in range(4):
         index = jnp.where(sub == j, hub_ref[j], index)
     hub = pick(index, 16)[:8]
 
-    slots_ref[...] = jnp.zeros(slots_ref.shape, f32)
+    for copy in copies[4:]:
+        copy.wait()
+    for b in range(own_blocks):
+        part = slice(b * TB, (b + 1) * TB)
+        weighted_ref[part] = (_column(root[b:b + 1]) * cotangent_ref[part].astype(f32)).astype(bf16)
     live = live_ref[0]
 
     def step(t):
@@ -68,9 +92,10 @@
             slots_ref[source_ref[t + k]] += jnp.where(t + k < live, products[k], 0.0)
 
     _tile_loop(live, step)
-    local_ref[...] = slots_ref[:own_blocks].reshape(own_blocks * TB, TB)
+    out.append(pltpu.make_async_copy(slots_ref.at[0:own_blocks], local_hbm, sems.at[11]))
+    out[-1].start()
     for i in range(bound_blocks):
-        send_ref[8 * i:8 * i + 8, 16:32, :] = slots_ref[own_blocks + i].astype(bf16).reshape(8, 16, TB)
+        late_ref[8 * i:8 * i + 8, 0:16, :] = slots_ref[own_blocks + i].astype(bf16).reshape(8, 16, TB)
     first = lax.broadcasted_iota(jnp.int32, (16, 8, TB), 1) < 4
     hub_tile = jnp.broadcast_to(hub[None], (16, 8, TB))
     for h in range(slots_ref.shape[0] - own_blocks - bound_blocks):
@@ -78,7 +103,11 @@
         odd = jnp.where(first, hub_tile, x)
         even = jnp.where(first, hub_tile, pltpu.roll(x, 4, 1))
         pair = jnp.stack([even, odd], axis=1).reshape(32, 8, TB)
-        send_ref[32 * h:32 * h + 32, 32:40, :] = pair.astype(bf16)
+        late_ref[32 * h:32 * h + 32, 16:24, :] = pair.astype(bf16)
+    out.append(pltpu.make_async_copy(late_ref, send_hbm.at[:, 16:40, :], sems.at[12]))
+    out[-1].start()
+    for copy in out:
+        copy.wait()
 
 
 def _after_kernel(live_ref, target_ref, source_ref, hub_ref, degrees_ref, rows_ref, arrived_ref, local_ref,
@@ -119,7 +148,7 @@
             [(jnp.broadcast_to(rows_ref[i:i + 1], (TB, TB)) == sub + b * TB).astype(f32).astype(bf16)
              for i in range(bound_blocks)], axis=1)
         part = slice(b * TB, (b + 1) * TB)
-        gradient_ref[part] = local_ref[part] + jnp.dot(onehot, returned, preferred_element_type=f32)
+        gradient_ref[part] = local_ref[b] + jnp.dot(onehot, returned, preferred_element_type=f32)
     for j in range(4):
         row = pl.ds(hub_ref[j], 1)
         gradient_ref[row, :] = gradient_ref[row, :] + hub_total[4 + j:5 + j]
@@ -148,28 +177,41 @@
     small = (live_tile_count.reshape(1), tile_target.reshape(slots), tile_source.reshape(slots), hub_rows.reshape(hubs))
     degree_blocks = degrees.reshape(own_blocks, TB)
     rows = send_rows.reshape(partitions * pair_rows // TB, TB)
+    rows_by_place = send_rows[0].T
     in_smem = pl.BlockSpec(memory_space=pltpu.SMEM)
+    in_hbm = pl.BlockSpec(memory_space=pltpu.HBM)
     in_vmem = pl.BlockSpec(memory_space=pltpu.VMEM)
+    shape = jax.ShapeDtypeStruct
     pair = 2 * (pair_rows + hubs)
+
+    def held(space, array):
+        return space(array.shape, array.dtype)
 
     send, local, scaled = pl.pallas_call(
         _before_kernel,
         out_shape=(
-            jax.ShapeDtypeStruct((partitions, pair, width), bf16),
-            jax.ShapeDtypeStruct((own_rows, width), f32),
-            jax.ShapeDtypeStruct((own_rows, width), bf16),
-        ),
-        in_specs=[in_smem] * 4 + [in_vmem] * 5,
-        out_specs=(in_vmem,) * 3,
-        scratch_shapes=[pltpu.VMEM((own_rows, width), bf16), pltpu.VMEM((source_blocks, TB, width), f32)],
+            shape((partitions, pair, width), bf16), shape((own_blocks, TB, width), f32),
+            shape((own_rows, width), bf16)),
+        in_specs=[in_hbm] * 9,
+        out_specs=(in_hbm,) * 3,
+        scratch_shapes=[held(pltpu.SMEM, x) for x in small] + [
+            held(pltpu.VMEM, x) for x in (degree_blocks, rows_by_place, embedding, cotangent, tiles)] + [
+            pltpu.VMEM((partitions, pair_rows, width), bf16),
+            pltpu.VMEM((partitions, pair - pair_rows, width), bf16),
+            pltpu.VMEM((own_rows, width), bf16),
+            pltpu.VMEM((own_rows, width), bf16),
+            pltpu.VMEM((source_blocks, TB, width), f32),
+            pltpu.VMEM((partitions * pair_rows, width), f32),
+            pltpu.SemaphoreType.DMA((13,)),
+        ],
         name="before",
-    )(*small, degree_blocks, rows, embedding, cotangent, tiles)
+    )(*small, degree_blocks, rows_by_place, embedding, cotangent, tiles)
 
     arrived = lax.all_to_all(send, "dom", split_axis=0, concat_axis=0, tiled=True)
 
     exchange = pl.pallas_call(
         _after_kernel,
-        out_shape=jax.ShapeDtypeStruct((replicas, 2 * own_rows // replicas, width), bf16),
+        out_shape=shape((replicas, 2 * own_rows // replicas, width), bf16),
         in_specs=[in_smem] * 4 + [in_vmem] * 6,
         out_specs=in_vmem,
         scratch_shapes=[
@@ -177,6 +219,7 @@
             pltpu.VMEM((own_blocks, TB, width), f32),
             pltpu.VMEM((own_rows, width), f32),
         ],
+        compiler_params=pltpu.CompilerParams(vmem_limit_bytes=20 << 20),
         name="after",
     )(*small, degree_blocks, rows, arrived, local, scaled, tiles)
 

time: 81.3 us -> 76.7 us (0.943)
  blocking collectives: 68.4 us -> 11.5 us
  waiting for transfers between devices: 0 us -> 35.8 us
  starting transfers between devices: 0 us -> 18.5 us
  Pallas kernels: 8.62 us -> 7.19 us
  local copies, waits for them, and re-layouts: 2.14 us -> 0.89 us
    all_to_all x1 -> x0, blocking collectives: 55.2 us -> none  [body(): lax.all_to_all(send, 'dom', split_axis=0, concat_axis=0, tiled=True)]
    all_to_all x0 -> x1, waiting for transfers between devices: none -> 35.8 us  [body(): lax.all_to_all(send, 'dom', split_axis=0, concat_axis=0, tiled=True)]
    all_to_all x0 -> x1, starting transfers between devices: none -> 18.5 us  [body(): lax.all_to_all(send, 'dom', split_axis=0, concat_axis=0, tiled=True)]
    all_to_all x1, blocking collectives: 13.1 us -> 11.5 us  [body(): lax.all_to_all(exchange, 'rep', split_axis=0, concat_axis=0, tiled=True)]
    pallas_call x2, Pallas kernels: 8.62 us -> 7.19 us  [the longest x1 4.44 us: body(): pl.pallas_call(_before_kernel, out_shape=(shape((partitions, pair, width)...]
  transfers between devices with their start and end apart: 0 -> 1, of which waited for: 0 -> 1; matrix products, arithmetic and copies ran while one was open for 0% -> 0% of each run, Pallas kernels for 0% -> 0%
where the time goes in v3:
time: 76.7 us; the launch traced here: 75.5 us
  waiting for transfers between devices  35.8 us (47%)
  starting transfers between devices  18.5 us (24%)
  blocking collectives  11.5 us (15%)
  Pallas kernels  7.19 us (9%)
  between operations  1.41 us (2%)
  local copies, waits for them, and re-layouts  0.89 us (1%)
    all_to_all x1, waiting for transfers between devices, body(): lax.all_to_all(send, 'dom', split_axis=0, concat_axis=0, tiled=True)  35.8 us
    all_to_all x1, starting transfers between devices, body(): lax.all_to_all(send, 'dom', split_axis=0, concat_axis=0, tiled=True)  18.5 us
    all_to_all x1, blocking collectives, body(): lax.all_to_all(exchange, 'rep', split_axis=0, concat_axis=0, tiled=True)  11.5 us
    pallas_call x1, Pallas kernels, body(): pl.pallas_call(_before_kernel, out_shape=(shape((partitions, pair, width)...  4.44 us
    pallas_call x1, Pallas kernels, body(): pl.pallas_call(_after_kernel, out_shape=shape((replicas, 2 * own_rows //...  2.75 us
  transfers between devices with their start and end apart: 1, of which 1 were waited for; matrix products, arithmetic and copies ran while one was open for 0% of the time, Pallas kernels for 0%

profile of v3, /device:TPU:1, one launch (start us, length us, event | category | flops | bytes accessed | tf_op | source)
XLA Modules:
  0.0 75.5 jit_solution(6139272995350700642)
XLA Ops:
  1.3 4.4 %before.1 = (bf16[128,40,128]{2,1,0:T(8,128)(2,1)}, f32[8,128,128]{2,1,0:T(8,128)}, bf16[1024,128]{1,0:T(8,128)(2,1)}) custom-call(s32[1]{0:T(128)} %bitcast.9.live_hbm, s32[32]{0:T(128)} %bitcast.15, s32[32]{0:T(128)} %bitcast.17, s32[4]{0:T(128)} %bitcast.19, s32[8,128]{1,0:T(8,128)} %bitcast.13, s32[16,128]{1,0:T(8,128)} %bitcast.21, ...), custom_call_target="tpu_custom_call" | custom-call | tf_op jit(solution)/shard_map/before/pallas_call | solution.py:190
  5.7 0.0 copy-start.7
  5.7 0.0 copy-start
  5.7 0.0 copy-start.1
  5.8 0.0 copy-start.2
  5.8 0.0 copy-start.3
  5.8 0.0 copy-start.4
  5.8 0.0 copy-start.5
  5.8 0.0 copy-start.6
  5.8 18.5 %all-to-all-start = ((bf16[128,40,128]{2,1,0:T(8,128)(2,1)}), bf16[128,40,128]{2,1,0:T(8,128)(2,1)S(1)}, u32[]{:S(2)}, u32[]{:S(2)}) async-start(bf16[128,40,128]{2,1,0:T(8,128)(2,1)} %get-tuple-element.5), calls=%async_computation | async-start | bytes 2621440 | tf_op jit(solution)/shard_map/all_to_all | solution.py:210
  24.4 0.0 copy-done.7
  24.4 0.1 copy.12
  24.5 0.1 reshape.30.rows_ref
  24.6 35.8 %all-to-all-done.arrived_ref = bf16[128,40,128]{2,1,0:T(8,128)(2,1)S(1)} async-done(((bf16[128,40,128]{2,1,0:T(8,128)(2,1)}), bf16[128,40,128]{2,1,0:T(8,128)(2,1)S(1)}, u32[]{:S(2)}, u32[]{:S(2)}) %all-to-all-start) | async-done | bytes 1310752 | tf_op jit(solution)/shard_map/all_to_all | solution.py:210
  60.4 0.0 copy-done
  60.4 0.0 copy-done.1
  60.4 0.0 copy-done.2
  60.4 0.0 copy-done.3
  60.4 0.0 copy-done.4
  60.4 0.0 copy-done.5
  60.5 0.0 copy-done.6
  60.5 2.7 %after.1 = bf16[4,512,128]{2,1,0:T(8,128)(2,1)S(1)} custom-call(s32[1]{0:T(128)} %bitcast.10.live_ref, s32[32]{0:T(128)S(1)} %bitcast.16, s32[32]{0:T(128)S(1)} %bitcast.18, s32[4]{0:T(128)S(1)} %bitcast.20, s32[8,128]{1,0:T(8,128)S(1)} %bitcast.14, s32[16,128]{1,0:T(8,128)S(1)} %reshape.30.rows_ref, bf16[128,40,128]{2,1,0:T(8,128)(2,1)S(1)} %all-to-all-done.arrived_ref, ...), custom_call_target="tpu_custom_call" | custom-call | tf_op jit(solution)/shard_map/after/pallas_call | solution.py:212
  63.2 11.5 %all_to_all.10 = bf16[4,512,128]{2,1,0:T(8,128)(2,1)S(1)} all-to-all(bf16[4,512,128]{2,1,0:T(8,128)(2,1)S(1)} %after.1), channel_id=1, replica_groups=mesh['dom'=128,'rep'=4] {'rep'}, dimensions={0} | all-to-all | bytes 1048576 | tf_op jit(solution)/shard_map/all_to_all | solution.py:226
  74.8 0.1 reduce_sum.12
  74.8 0.7 fusion
Async XLA Ops:
  5.7 18.7 %copy-start.7 = (s32[1,128,16]{1,2,0:T(8,128)S(1)}, s32[1,128,16]{1,2,0:T(8,128)}, u32[]{:S(2)}) copy-start(s32[1,128,16]{1,2,0:T(8,128)} %param.16) | copy-start | bytes 24580
  5.7 54.7 %copy-start = (bf16[1,1,32,128,128]{4,3,2,1,0:T(8,128)(2,1)S(1)}, bf16[1,1,32,128,128]{4,3,2,1,0:T(8,128)(2,1)}, u32[]{:S(2)}) copy-start(bf16[1,1,32,128,128]{4,3,2,1,0:T(8,128)(2,1)} %param.12) | copy-start | bytes 3145732
  5.7 54.7 %copy-start.1 = (f32[8,128,128]{2,1,0:T(8,128)S(1)}, f32[8,128,128]{2,1,0:T(8,128)}, u32[]{:S(2)}) copy-start(f32[8,128,128]{2,1,0:T(8,128)} %get-tuple-element.6.local_ref) | copy-start | bytes 1572868
  5.8 54.7 %copy-start.2 = (bf16[1024,128]{1,0:T(8,128)(2,1)S(1)}, bf16[1024,128]{1,0:T(8,128)(2,1)}, u32[]{:S(2)}) copy-start(bf16[1024,128]{1,0:T(8,128)(2,1)} %get-tuple-element.7.scaled_ref) | copy-start | bytes 786436
  5.8 54.7 %copy-start.3 = (s32[1024]{0:T(1024)S(1)}, s32[1024]{0:T(1024)}, u32[]{:S(2)}) copy-start(s32[1024]{0:T(1024)} %param.11) | copy-start | bytes 12292
  5.8 54.7 %copy-start.4 = (s32[1,1,32]{2,1,0:T(1,128)S(1)}, s32[1,1,32]{2,1,0:T(1,128)}, u32[]{:S(2)}) copy-start(s32[1,1,32]{2,1,0:T(1,128)} %param.13) | copy-start | bytes 388
  5.8 54.7 %copy-start.5 = (s32[1,1,32]{2,1,0:T(1,128)S(1)}, s32[1,1,32]{2,1,0:T(1,128)}, u32[]{:S(2)}) copy-start(s32[1,1,32]{2,1,0:T(1,128)} %param.14) | copy-start | bytes 388
  5.8 54.7 %copy-start.6 = (s32[1,4]{1,0:T(1,128)S(1)}, s32[1,4]{1,0:T(1,128)}, u32[]{:S(2)}) copy-start(s32[1,4]{1,0:T(1,128)} %param.17) | copy-start | bytes 52
  5.8 54.6 %all-to-all-start = ((bf16[128,40,128]{2,1,0:T(8,128)(2,1)}), bf16[128,40,128]{2,1,0:T(8,128)(2,1)S(1)}, u32[]{:S(2)}, u32[]{:S(2)}) async-start(bf16[128,40,128]{2,1,0:T(8,128)(2,1)} %get-tuple-element.5), calls=%async_computation | async-start | bytes 2621440 | tf_op jit(solution)/shard_map/all_to_all | solution.py:210

commit v4 on v3

--- a/solution.py
+++ b/solution.py
@@ -6,7 +6,7 @@
 from jax.sharding import PartitionSpec as P
 
 TB = 128
-GROUP = 4
+GROUP = 16
 
 
 def _column(row):

time: 76.7 us -> 76.3 us (level)
  Pallas kernels: 7.19 us -> 6.19 us
  blocking collectives: 11.5 us -> 12.4 us
    all_to_all x1, blocking collectives: 11.5 us -> 12.4 us  [body(): lax.all_to_all(exchange, 'rep', split_axis=0, concat_axis=0, tiled=True)]
where the time goes in v4:
time: 76.3 us; the launch traced here: 75.4 us
  waiting for transfers between devices  35.8 us (47%)
  starting transfers between devices  18.6 us (24%)
  blocking collectives  12.4 us (16%)
  Pallas kernels  6.19 us (8%)
  between operations  1.41 us (2%)
  local copies, waits for them, and re-layouts  0.89 us (1%)
    all_to_all x1, waiting for transfers between devices, body(): lax.all_to_all(send, 'dom', split_axis=0, concat_axis=0, tiled=True)  35.8 us
    all_to_all x1, starting transfers between devices, body(): lax.all_to_all(send, 'dom', split_axis=0, concat_axis=0, tiled=True)  18.6 us
    all_to_all x1, blocking collectives, body(): lax.all_to_all(exchange, 'rep', split_axis=0, concat_axis=0, tiled=True)  12.4 us
    pallas_call x1, Pallas kernels, body(): pl.pallas_call(_before_kernel, out_shape=(shape((partitions, pair, width)...  3.89 us
    pallas_call x1, Pallas kernels, body(): pl.pallas_call(_after_kernel, out_shape=shape((replicas, 2 * own_rows //...  2.3 us
  transfers between devices with their start and end apart: 1, of which 1 were waited for; matrix products, arithmetic and copies ran while one was open for 0% of the time, Pallas kernels for 0%

profile of v4, /device:TPU:1, one launch (start us, length us, event | category | flops | bytes accessed | tf_op | source)
XLA Modules:
  0.0 75.4 jit_solution(16699593247675708521)
XLA Ops:
  1.3 3.9 %before.1 = (bf16[128,40,128]{2,1,0:T(8,128)(2,1)}, f32[8,128,128]{2,1,0:T(8,128)}, bf16[1024,128]{1,0:T(8,128)(2,1)}) custom-call(s32[1]{0:T(128)} %bitcast.9.live_hbm, s32[32]{0:T(128)} %bitcast.15, s32[32]{0:T(128)} %bitcast.17, s32[4]{0:T(128)} %bitcast.19, s32[8,128]{1,0:T(8,128)} %bitcast.13, s32[16,128]{1,0:T(8,128)} %bitcast.21, ...), custom_call_target="tpu_custom_call" | custom-call | tf_op jit(solution)/shard_map/before/pallas_call | solution.py:190
  5.2 0.0 copy-start.7
  5.2 0.0 copy-start
  5.2 0.0 copy-start.1
  5.2 0.0 copy-start.2
  5.2 0.0 copy-start.3
  5.2 0.0 copy-start.4
  5.2 0.0 copy-start.5
  5.3 0.0 copy-start.6
  5.3 18.6 %all-to-all-start = ((bf16[128,40,128]{2,1,0:T(8,128)(2,1)}), bf16[128,40,128]{2,1,0:T(8,128)(2,1)S(1)}, u32[]{:S(2)}, u32[]{:S(2)}) async-start(bf16[128,40,128]{2,1,0:T(8,128)(2,1)} %get-tuple-element.5), calls=%async_computation | async-start | bytes 2621440 | tf_op jit(solution)/shard_map/all_to_all | solution.py:210
  23.8 0.0 copy-done.7
  23.8 0.1 copy.12
  23.9 0.1 reshape.30.rows_ref
  24.0 35.8 %all-to-all-done.arrived_ref = bf16[128,40,128]{2,1,0:T(8,128)(2,1)S(1)} async-done(((bf16[128,40,128]{2,1,0:T(8,128)(2,1)}), bf16[128,40,128]{2,1,0:T(8,128)(2,1)S(1)}, u32[]{:S(2)}, u32[]{:S(2)}) %all-to-all-start) | async-done | bytes 1310752 | tf_op jit(solution)/shard_map/all_to_all | solution.py:210
  59.9 0.0 copy-done
  59.9 0.0 copy-done.1
  59.9 0.0 copy-done.2
  59.9 0.0 copy-done.3
  59.9 0.0 copy-done.4
  59.9 0.0 copy-done.5
  59.9 0.0 copy-done.6
  59.9 2.3 %after.1 = bf16[4,512,128]{2,1,0:T(8,128)(2,1)S(1)} custom-call(s32[1]{0:T(128)} %bitcast.10.live_ref, s32[32]{0:T(128)S(1)} %bitcast.16, s32[32]{0:T(128)S(1)} %bitcast.18, s32[4]{0:T(128)S(1)} %bitcast.20, s32[8,128]{1,0:T(8,128)S(1)} %bitcast.14, s32[16,128]{1,0:T(8,128)S(1)} %reshape.30.rows_ref, bf16[128,40,128]{2,1,0:T(8,128)(2,1)S(1)} %all-to-all-done.arrived_ref, ...), custom_call_target="tpu_custom_call" | custom-call | tf_op jit(solution)/shard_map/after/pallas_call | solution.py:212
  62.2 12.4 %all_to_all.10 = bf16[4,512,128]{2,1,0:T(8,128)(2,1)S(1)} all-to-all(bf16[4,512,128]{2,1,0:T(8,128)(2,1)S(1)} %after.1), channel_id=1, replica_groups=mesh['dom'=128,'rep'=4] {'rep'}, dimensions={0} | all-to-all | bytes 1048576 | tf_op jit(solution)/shard_map/all_to_all | solution.py:226
  74.6 0.1 reduce_sum.12
  74.7 0.7 fusion
Async XLA Ops:
  5.2 18.7 %copy-start.7 = (s32[1,128,16]{1,2,0:T(8,128)S(1)}, s32[1,128,16]{1,2,0:T(8,128)}, u32[]{:S(2)}) copy-start(s32[1,128,16]{1,2,0:T(8,128)} %param.16) | copy-start | bytes 24580
  5.2 54.7 %copy-start = (bf16[1,1,32,128,128]{4,3,2,1,0:T(8,128)(2,1)S(1)}, bf16[1,1,32,128,128]{4,3,2,1,0:T(8,128)(2,1)}, u32[]{:S(2)}) copy-start(bf16[1,1,32,128,128]{4,3,2,1,0:T(8,128)(2,1)} %param.12) | copy-start | bytes 3145732
  5.2 54.7 %copy-start.1 = (f32[8,128,128]{2,1,0:T(8,128)S(1)}, f32[8,128,128]{2,1,0:T(8,128)}, u32[]{:S(2)}) copy-start(f32[8,128,128]{2,1,0:T(8,128)} %get-tuple-element.6.local_ref) | copy-start | bytes 1572868
  5.2 54.7 %copy-start.2 = (bf16[1024,128]{1,0:T(8,128)(2,1)S(1)}, bf16[1024,128]{1,0:T(8,128)(2,1)}, u32[]{:S(2)}) copy-start(bf16[1024,128]{1,0:T(8,128)(2,1)} %get-tuple-element.7.scaled_ref) | copy-start | bytes 786436
  5.2 54.7 %copy-start.3 = (s32[1024]{0:T(1024)S(1)}, s32[1024]{0:T(1024)}, u32[]{:S(2)}) copy-start(s32[1024]{0:T(1024)} %param.11) | copy-start | bytes 12292
  5.2 54.7 %copy-start.4 = (s32[1,1,32]{2,1,0:T(1,128)S(1)}, s32[1,1,32]{2,1,0:T(1,128)}, u32[]{:S(2)}) copy-start(s32[1,1,32]{2,1,0:T(1,128)} %param.13) | copy-start | bytes 388
  5.2 54.7 %copy-start.5 = (s32[1,1,32]{2,1,0:T(1,128)S(1)}, s32[1,1,32]{2,1,0:T(1,128)}, u32[]{:S(2)}) copy-start(s32[1,1,32]{2,1,0:T(1,128)} %param.14) | copy-start | bytes 388
  5.3 54.7 %copy-start.6 = (s32[1,4]{1,0:T(1,128)S(1)}, s32[1,4]{1,0:T(1,128)}, u32[]{:S(2)}) copy-start(s32[1,4]{1,0:T(1,128)} %param.17) | copy-start | bytes 52
  5.3 54.6 %all-to-all-start = ((bf16[128,40,128]{2,1,0:T(8,128)(2,1)}), bf16[128,40,128]{2,1,0:T(8,128)(2,1)S(1)}, u32[]{:S(2)}, u32[]{:S(2)}) async-start(bf16[128,40,128]{2,1,0:T(8,128)(2,1)} %get-tuple-element.5), calls=%async_computation | async-start | bytes 2621440 | tf_op jit(solution)/shard_map/all_to_all | solution.py:210
